TPU v7x, 128 devices: a whole 4x4x4 slice. The times are simulated.
128 devices in a mesh: slab: 4 (over x), member: 32 (over y, z, core).
Axes of the slice: x: 4, y: 4, z: 4, core: 2. Of those that a mesh axis runs over, the one named last changes fastest.
Arguments:
- initial: float32 [256, 512, 1024], P('member', 'slab'), may hold values from -6 to 6
- stencil_numbers: float32 [3, 512, 1024], P(None, 'slab'), may hold values from -0.25 to 0.25, as said below
- innovations: float32 [256, 131072], P(None, ('slab', 'member')), may hold values from -6 to 6
- obs_prec: float32 [131072], P(('slab', 'member')), may hold values from 0.05 to 0.5
- obs_cell: int32 [4096, 32], P(('slab', 'member')), may hold values from 0 to 127
- band_idx: int32 [4096, 9], P(('slab', 'member')), may hold values from 0 to 4095, as said below
Outputs:
- analysis: float32 [256, 512, 1024], P('member', 'slab')
Inputs may be any that keep to these rules, and one draw needn't show every extreme that they name: stencil_numbers[0] lies in 0.08 to 0.2; stencil_numbers[1] and stencil_numbers[2] lie in -0.25 to 0.25. `band_idx`: row b holds 9 distinct block indices j with |j - b| <= 8.
All inputs are finite; a program needn't handle non-finite values.
Results may differ from a plain program's by a relative error of at most 0.00011.
Values sent between devices are 32-bit elements; how exact they have to be, the bound alone decides.
A program may use at most 128 MiB of HBM per device.

v0:
```python
import functools

import jax
import jax.numpy as jnp
from jax import lax
from jax.experimental import pallas as pl
from jax.experimental.pallas import tpu as pltpu
from jax.sharding import PartitionSpec as P

MESH = pl.DeviceIdType.MESH
F32 = jnp.float32
BF16 = jnp.bfloat16
OB = 32
R = 8
SLABS = 4
GROUPS = 32
CHIPS = 16
ROWS = 128
LON = 1024
MEM = 8
MEMBERS = 256
TILE_ROWS = 4
ROW_BLOCKS = 8
TILE_BLOCKS = 32
ROW_OBS = ROW_BLOCKS * OB


def split(value):
    high = value.astype(BF16)
    low = (value - high.astype(F32)).astype(BF16)
    return high, low


def dot3(a_high, a_low, b_high, b_low):
    dot = functools.partial(jnp.dot, preferred_element_type=F32)
    return dot(a_high, b_high) + dot(a_high, b_low) + dot(a_low, b_high)


def dot_t(a, b):
    return lax.dot_general(a, b, (((1,), (1,)), ((), ())), preferred_element_type=F32)


def cycle_kernel(
    init_ref, sten_ref, inn_ref, prec_ref, cell_ref, band_ref, ret_ref,
    xbuf, xt, sten, coef, step_a, step_b, fsend, fields, anom_high, anom_low,
    pick, obs, obs_high, obs_low, wgt, wgt_high, wgt_low, inn, taper, upd,
    load_sem, halo_send, halo_recv, fwd_send, fwd_recv, own_sem, rim_send, rim_recv, ret_send, ret_recv,
):
    s = lax.axis_index("slab")
    g = lax.axis_index("member")
    chip = g // 2
    core = g % 2
    flat = s * GROUPS + g
    up = lax.rem(s + 1, SLABS)
    down = lax.rem(s + SLABS - 1, SLABS)
    nxt = lax.rem(flat + 1, SLABS * GROUPS)
    prv = lax.rem(flat + SLABS * GROUPS - 1, SLABS * GROUPS)
    nxt_id = (nxt // GROUPS, lax.rem(nxt, GROUPS))
    prv_id = (prv // GROUPS, lax.rem(prv, GROUPS))

    barrier = pltpu.get_barrier_semaphore()

    def greet(i, carry):
        peer = lax.rem(g + i, GROUPS)
        pl.semaphore_signal(barrier, inc=1, device_id=(s, peer), device_id_type=MESH)
        return carry

    for device in ((up, g), (down, g), nxt_id, prv_id):
        pl.semaphore_signal(barrier, inc=1, device_id=device, device_id_type=MESH)
    lax.fori_loop(1, GROUPS, greet, 0)

    load_x = pltpu.make_async_copy(init_ref, xbuf, load_sem.at[0])
    load_s = pltpu.make_async_copy(sten_ref, sten.at[:, pl.ds(8, ROWS), :], load_sem.at[1])
    load_i = pltpu.make_async_copy(inn_ref, inn, load_sem.at[2])
    load_x.start()
    load_s.start()
    load_i.start()

    load_x.wait()

    def turn(k, carry):
        start = pl.multiple_of(k * 8, 8)
        rows = xbuf[:, pl.ds(start, 8), :]
        xt[pl.ds(k * 8 + 4, 8)] = jnp.swapaxes(rows, 0, 1)
        return carry

    turn(0, 0)
    turn(CHIPS - 1, 0)

    pl.semaphore_wait(barrier, GROUPS - 1 + 4)

    def remote(src, dst, send_sem, recv_sem, device):
        return pltpu.make_async_remote_copy(
            src_ref=src, dst_ref=dst, send_sem=send_sem, recv_sem=recv_sem,
            device_id=device, device_id_type=MESH,
        )

    halos = [
        remote(sten_ref.at[:, pl.ds(ROWS - 8, 8), :], sten.at[:, pl.ds(0, 8), :], halo_send.at[0], halo_recv.at[0], (up, g)),
        remote(sten_ref.at[:, pl.ds(0, 8), :], sten.at[:, pl.ds(ROWS + 8, 8), :], halo_send.at[1], halo_recv.at[1], (down, g)),
        remote(xt.at[pl.ds(ROWS, 4)], xt.at[pl.ds(0, 4)], halo_send.at[2], halo_recv.at[2], (up, g)),
        remote(xt.at[pl.ds(4, 4)], xt.at[pl.ds(ROWS + 4, 4)], halo_send.at[3], halo_recv.at[3], (down, g)),
    ]
    for copy in halos:
        copy.start()

    lax.fori_loop(1, CHIPS - 1, turn, 0)

    def coefficients(start, live):
        rows = pl.ds(start, 8)
        k = sten[0, rows, :] * live
        u = sten[1, rows, :] * (0.5 * live)
        v = sten[2, rows, :] * (0.5 * live)
        coef[0, rows, :] = 1.0 - 4.0 * k
        coef[1, rows, :] = k - u
        coef[2, rows, :] = k + u
        coef[3, rows, :] = k - v
        coef[4, rows, :] = k + v

    load_s.wait()

    def own_coefficients(t, carry):
        coefficients(pl.multiple_of(t * 8 + 8, 8), 1.0)
        return carry

    lax.fori_loop(0, CHIPS, own_coefficients, 0)

    def target(i):
        return lax.rem(chip + 7 * i, CHIPS)

    def early_target(i):
        k = target(i)
        edge = 1 - (lax.rem(k + 1, CHIPS) + 14) // 16
        middle = 1 - (lax.rem(k + 9, CHIPS) + 14) // 16
        first = 1 - (i + 11) // 16
        later = ((i + 7) // 16) * (1 - (i + 3) // 16)
        return lax.rem(k + 8 * (first * edge + later * middle), CHIPS)

    def advance(src, src_start, dst, dst_start, count, coef_base, coef_offset):
        for row in range(count):
            centre = src[src_start + row + 1]
            north = src[src_start + row + 2]
            south = src[src_start + row]
            east = pltpu.roll(centre, LON - 1, 1)
            west = pltpu.roll(centre, 1, 1)
            at = pl.ds(coef_base + coef_offset + row, 1)
            dst[dst_start + row] = (
                coef[0, at, :] * centre
                + coef[1, at, :] * east
                + coef[2, at, :] * west
                + coef[3, at, :] * north
                + coef[4, at, :] * south
            )

    def forecast(k):
        base = pl.multiple_of(k * 8, 8)
        advance(xt, k * 8, step_a, 0, 14, base, 5)
        advance(step_a, 0, step_b, 0, 12, base, 6)
        advance(step_b, 0, step_a, 0, 10, base, 7)
        advance(step_a, 0, fsend, k * 8, 8, base, 8)

    def send_rows(k, c, row, count, sem):
        remote(
            fsend.at[pl.ds(k * 8 + 4 * c + row, count)],
            fields.at[pl.ds(row, count), pl.ds(pl.multiple_of(g * MEM, MEM), MEM), :],
            fwd_send, sem, (s, 2 * k + c),
        ).start()

    def first_rows(i, carry):
        @pl.when(i == 5)
        def _():
            for copy in halos:
                copy.wait()
            coefficients(0, jnp.where(s == 0, 0.0, 1.0).astype(F32))
            coefficients(ROWS + 8, jnp.where(s == SLABS - 1, 0.0, 1.0).astype(F32))

            @pl.when(s == 0)
            def _():
                xt[pl.ds(0, 4)] = jnp.zeros((4, MEM, LON), F32)

            @pl.when(s == SLABS - 1)
            def _():
                xt[pl.ds(ROWS + 4, 4)] = jnp.zeros((4, MEM, LON), F32)

        k = early_target(i)
        forecast(k)
        for c in range(2):
            send_rows(k, c, 0, 2, fwd_recv.at[0])
        return carry

    lax.fori_loop(1, CHIPS, first_rows, 0)
    forecast(chip)
    send_rows(chip, 1 - core, 0, 2, fwd_recv.at[0])
    own = pltpu.make_async_copy(
        fsend.at[pl.ds(g * 4, 4)], fields.at[:, pl.ds(pl.multiple_of(g * MEM, MEM), MEM), :], own_sem.at[0]
    )
    own.start()

    for row in (2, 3):
        def later_rows(i, carry, row=row):
            k = target(i)
            for c in range(2):
                send_rows(k, c, row, 1, fwd_recv.at[row - 1])
            return carry

        lax.fori_loop(1, CHIPS, later_rows, 0)
        send_rows(chip, 1 - core, row, 1, fwd_recv.at[row - 1])

    load_i.wait()
    scale = 1.0 / ((R + 1.0) * (MEMBERS - 1.0))
    for row in range(TILE_ROWS):
        cols = pl.ds(row * ROW_OBS, ROW_OBS)
        wgt[row + 1] = inn[:, cols] * (prec_ref[:, cols] * scale)

    def split_weights(slot):
        wgt_high[slot], wgt_low[slot] = split(wgt[slot])

    def split_observed(slot):
        obs_high[slot], obs_low[slot] = split(obs[slot])

    rim_w = [
        remote(wgt.at[TILE_ROWS], wgt.at[0], rim_send.at[0], rim_recv.at[0], nxt_id),
        remote(wgt.at[1], wgt.at[TILE_ROWS + 1], rim_send.at[1], rim_recv.at[1], prv_id),
    ]
    for copy in rim_w:
        copy.start()
    rim_o = [
        remote(obs.at[TILE_ROWS], obs.at[0], rim_send.at[2], rim_recv.at[2], nxt_id),
        remote(obs.at[1], obs.at[TILE_ROWS + 1], rim_send.at[3], rim_recv.at[3], prv_id),
    ]

    for row in range(TILE_ROWS):
        split_weights(row + 1)

    lane = lax.broadcasted_iota(jnp.int32, (OB, 128), 1)
    for b in range(TILE_BLOCKS):
        pick[b] = jnp.where(lane == cell_ref[:, b : b + 1], 1.0, 0.0).astype(BF16)

    block = lax.broadcasted_iota(jnp.int32, (TILE_BLOCKS, 128), 0)
    slot_lane = lax.broadcasted_iota(jnp.int32, (TILE_BLOCKS, 128), 1)
    here = flat * TILE_BLOCKS + block
    row_start = flat * TILE_BLOCKS + jnp.bitwise_and(block, -8) - R
    total = jnp.zeros((TILE_BLOCKS, 128), F32)
    for n in range(R + 1):
        member_of = band_ref[:, n : n + 1]
        height = (R + 1.0) - jnp.abs(member_of - here).astype(F32)
        total = total + jnp.where(slot_lane == member_of - row_start, height, 0.0)
    taper[...] = total

    own.wait()

    def prepare(row):
        def columns(c, carry):
            cols = pl.ds(pl.multiple_of(c * 256, 256), 256)
            field = fields[row, :, cols]
            mean = jnp.sum(field, axis=0, keepdims=True) * (1.0 / MEMBERS)
            high, low = split(field - mean)
            anom_high[row, :, cols] = high
            anom_low[row, :, cols] = low
            for b in range(2):
                pair = pl.ds(pl.multiple_of(c * 64 + b * OB, OB), OB)
                chosen = pick[row * ROW_BLOCKS + c * 2 + b]
                part = slice(b * 128, b * 128 + 128)
                obs[row + 1, pair, :] = dot_t(chosen, high[:, part]) + dot_t(chosen, low[:, part])
            return carry

        lax.fori_loop(0, 4, columns, 0)
        split_observed(row + 1)

    def arrived(row, count, sem):
        view = fields.at[pl.ds(row, count), pl.ds(0, MEMBERS - MEM), :]
        pltpu.make_async_copy(view, view, sem).wait()

    def analyse(row):
        def columns(c, carry):
            cols = pl.ds(pl.multiple_of(c * 256, 256), 256)
            high = anom_high[row, :, cols]
            low = anom_low[row, :, cols]
            weights = [taper[pl.ds(row * ROW_BLOCKS + c * 2 + b, 1), :] for b in range(2)]
            total = fields[row, :, cols]
            for part in range(3):
                slot = row + part
                cross = dot3(obs_high[slot], obs_low[slot], high, low)
                spread = jnp.concatenate(
                    [
                        jnp.concatenate(
                            [
                                jnp.broadcast_to(weights[b][:, part * 8 + j : part * 8 + j + 1], (OB, 128))
                                for b in range(2)
                            ],
                            axis=1,
                        )
                        for j in range(8)
                    ],
                    axis=0,
                )
                cross_high, cross_low = split(cross * spread)
                total = total + dot3(wgt_high[slot], wgt_low[slot], cross_high, cross_low)
            upd[row, :, cols] = total
            return carry

        lax.fori_loop(0, 4, columns, 0)

    def give_back(row):
        def one(k, c):
            d = 2 * k + c
            remote(
                upd.at[row, pl.ds(pl.multiple_of(d * MEM, MEM), MEM), :], ret_ref.at[TILE_ROWS * g + row],
                ret_send, ret_recv, (s, d),
            ).start()

        def others(i, carry):
            k = target(i)
            for c in range(2):
                one(k, c)
            return carry

        lax.fori_loop(1, CHIPS, others, 0)
        one(chip, 1 - core)

    arrived(0, 2, fwd_recv.at[0])
    prepare(0)
    rim_o[1].start()
    prepare(1)
    arrived(2, 1, fwd_recv.at[1])
    prepare(2)

    def finish(t, carry):
        row = lax.rem(t + 1, TILE_ROWS)

        @pl.when(t == 1)
        def _():
            arrived(3, 1, fwd_recv.at[2])
            prepare(3)
            rim_o[0].start()

        @pl.when(t == 2)
        def _():
            rim_w[1].wait_recv()
            rim_o[1].wait_recv()
            split_weights(TILE_ROWS + 1)
            split_observed(TILE_ROWS + 1)

        @pl.when(t == 3)
        def _():
            rim_w[0].wait_recv()
            rim_o[0].wait_recv()
            split_weights(0)
            split_observed(0)

        analyse(row)
        give_back(row)
        return carry

    lax.fori_loop(0, TILE_ROWS, finish, 0)

    keep = pltpu.make_async_copy(
        upd.at[:, pl.ds(pl.multiple_of(g * MEM, MEM), MEM), :], ret_ref.at[pl.ds(TILE_ROWS * g, TILE_ROWS)], own_sem.at[1]
    )
    keep.start()
    for copy in rim_w + rim_o:
        copy.wait_send()
    sent = fsend.at[pl.ds(0, ROWS - 4)]
    pltpu.make_async_copy(sent, sent, fwd_send).wait()
    keep.wait()
    back = ret_ref.at[pl.ds(0, ROWS - 4)]
    pltpu.make_async_copy(back, back, ret_send).wait()
    pltpu.make_async_copy(back, back, ret_recv).wait()


def turn_kernel(rows_ref, out_ref):
    out_ref[...] = jnp.swapaxes(rows_ref[...], 0, 1)


def shards(initial, stencil_numbers, innovations, obs_prec, obs_cell, band_idx):
    vmem = pl.BlockSpec(memory_space=pltpu.VMEM)
    hbm = pl.BlockSpec(memory_space=pl.ANY)
    dma = pltpu.SemaphoreType.DMA
    rows = pl.pallas_call(
        cycle_kernel,
        out_shape=jax.ShapeDtypeStruct((ROWS, MEM, LON), F32),
        in_specs=[hbm, hbm, hbm, vmem, vmem, vmem],
        out_specs=hbm,
        scratch_shapes=[
            pltpu.VMEM((MEM, ROWS, LON), F32),
            pltpu.VMEM((ROWS + 8, MEM, LON), F32),
            pltpu.VMEM((3, ROWS + 16, LON), F32),
            pltpu.VMEM((5, ROWS + 16, LON), F32),
            pltpu.VMEM((14, MEM, LON), F32),
            pltpu.VMEM((14, MEM, LON), F32),
            pltpu.VMEM((ROWS, MEM, LON), F32),
            pltpu.VMEM((TILE_ROWS, MEMBERS, LON), F32),
            pltpu.VMEM((TILE_ROWS, MEMBERS, LON), BF16),
            pltpu.VMEM((TILE_ROWS, MEMBERS, LON), BF16),
            pltpu.VMEM((TILE_BLOCKS, OB, 128), BF16),
            pltpu.VMEM((TILE_ROWS + 2, ROW_OBS, MEMBERS), F32),
            pltpu.VMEM((TILE_ROWS + 2, ROW_OBS, MEMBERS), BF16),
            pltpu.VMEM((TILE_ROWS + 2, ROW_OBS, MEMBERS), BF16),
            pltpu.VMEM((TILE_ROWS + 2, MEMBERS, ROW_OBS), F32),
            pltpu.VMEM((TILE_ROWS + 2, MEMBERS, ROW_OBS), BF16),
            pltpu.VMEM((TILE_ROWS + 2, MEMBERS, ROW_OBS), BF16),
            pltpu.VMEM((MEMBERS, TILE_ROWS * ROW_OBS), F32),
            pltpu.VMEM((TILE_BLOCKS, 128), F32),
            pltpu.VMEM((TILE_ROWS, MEMBERS, LON), F32),
            dma((3,)),
            dma((4,)),
            dma((4,)),
            dma(()),
            dma((3,)),
            dma((2,)),
            dma((4,)),
            dma((4,)),
            dma(()),
            dma(()),
        ],
        compiler_params=pltpu.CompilerParams(
            collective_id=0, has_side_effects=True, vmem_limit_bytes=60 * 2**20
        ),
        name="cycle",
    )(initial, stencil_numbers, innovations, obs_prec.reshape(1, -1), obs_cell.T, band_idx)
    group = 32
    return pl.pallas_call(
        turn_kernel,
        grid=(ROWS // group,),
        out_shape=jax.ShapeDtypeStruct((MEM, ROWS, LON), F32),
        in_specs=[pl.BlockSpec((group, MEM, LON), lambda i: (i, 0, 0))],
        out_specs=pl.BlockSpec((MEM, group, LON), lambda i: (0, i, 0)),
        compiler_params=pltpu.CompilerParams(vmem_limit_bytes=32 * 2**20),
        name="turn",
    )(rows)


def solution(mesh):
    in_specs = (
        P("member", "slab", None),
        P(None, "slab", None),
        P(None, ("slab", "member")),
        P(("slab", "member")),
        P(("slab", "member"), None),
        P(("slab", "member"), None),
    )
    out_specs = P("member", "slab", None)
    return jax.shard_map(shards, mesh=mesh, in_specs=in_specs, out_specs=out_specs, check_vma=False)
```

profile of v0, /device:TPU:17, one launch (start us, length us, event | category | flops | bytes accessed | tf_op | source)
XLA Modules:
  0.0 140.3 jit_solution(2943456780249381917)
XLA Ops:
  0.0 1.4 copy.7
  1.4 1.4 copy.8.band_ref
  2.8 132.6 %cycle.1.rows_ref = f32[128,8,1024]{2,1,0:T(8,128)} custom-call(f32[8,128,1024]{2,1,0:T(8,128)} %init_ref.1, f32[3,128,1024]{2,1,0:T(8,128)} %sten_ref.1, f32[256,1024]{1,0:T(8,128)} %inn_ref.1, f32[1,1024]{1,0:T(1,128)} %bitcast.3, s32[32,32]{1,0:T(8,128)} %bitcast.2, s32[32,9]{1,0:T(8,128)} %copy.8.band_ref), custom_call_target="tpu_custom_call" | custom-call | tf_op jit(solution)/shard_map/cycle/pallas_call | solution.py:379
  135.4 0.0 copy-start
  135.4 2.2 %copy-done = f32[128,8,1024]{2,1,0:T(8,128)S(1)} copy-done((f32[128,8,1024]{2,1,0:T(8,128)S(1)}, f32[128,8,1024]{2,1,0:T(8,128)}, u32[]{:S(2)}) %copy-start) | copy-done | bytes 4194328
  137.6 2.7 %turn.1 = f32[8,128,1024]{2,1,0:T(8,128)} custom-call(f32[128,8,1024]{2,1,0:T(8,128)S(1)} %copy-done), custom_call_target="tpu_custom_call" | custom-call | tf_op jit(solution)/shard_map/turn/pallas_call | solution.py:422
Async XLA Ops:
  135.4 2.2 %copy-start = (f32[128,8,1024]{2,1,0:T(8,128)S(1)}, f32[128,8,1024]{2,1,0:T(8,128)}, u32[]{:S(2)}) copy-start(f32[128,8,1024]{2,1,0:T(8,128)} %cycle.1.rows_ref) | copy-start | bytes 12582916
where the time goes:
time: 141 us; the launch traced here: 140 us
  Pallas kernels  135 us (96%)
  local copies, waits for them, and re-layouts  4.95 us (4%)
    pallas_call x1, Pallas kernels, shards(): pl.pallas_call(cycle_kernel, out_shape=jax.ShapeDtypeStruct((ROWS, MEM, L...  133 us
    unnamed x4, local copies, waits for them, and re-layouts  4.95 us

commit v1 on v0

--- a/solution.py
+++ b/solution.py
@@ -43,7 +43,7 @@
 def cycle_kernel(
     init_ref, sten_ref, inn_ref, prec_ref, cell_ref, band_ref, ret_ref,
     xbuf, xt, sten, coef, step_a, step_b, fsend, fields, anom_high, anom_low,
-    pick, obs, obs_high, obs_low, wgt, wgt_high, wgt_low, inn, taper, upd,
+    pick, obs, obs_high, obs_low, wgt, wgt_high, wgt_low, inn, square, taper, upd,
     load_sem, halo_send, halo_recv, fwd_send, fwd_recv, own_sem, rim_send, rim_recv, ret_send, ret_recv,
 ):
     s = lax.axis_index("slab")
@@ -84,27 +84,7 @@
         xt[pl.ds(k * 8 + 4, 8)] = jnp.swapaxes(rows, 0, 1)
         return carry
 
-    turn(0, 0)
-    turn(CHIPS - 1, 0)
-
-    pl.semaphore_wait(barrier, GROUPS - 1 + 4)
-
-    def remote(src, dst, send_sem, recv_sem, device):
-        return pltpu.make_async_remote_copy(
-            src_ref=src, dst_ref=dst, send_sem=send_sem, recv_sem=recv_sem,
-            device_id=device, device_id_type=MESH,
-        )
-
-    halos = [
-        remote(sten_ref.at[:, pl.ds(ROWS - 8, 8), :], sten.at[:, pl.ds(0, 8), :], halo_send.at[0], halo_recv.at[0], (up, g)),
-        remote(sten_ref.at[:, pl.ds(0, 8), :], sten.at[:, pl.ds(ROWS + 8, 8), :], halo_send.at[1], halo_recv.at[1], (down, g)),
-        remote(xt.at[pl.ds(ROWS, 4)], xt.at[pl.ds(0, 4)], halo_send.at[2], halo_recv.at[2], (up, g)),
-        remote(xt.at[pl.ds(4, 4)], xt.at[pl.ds(ROWS + 4, 4)], halo_send.at[3], halo_recv.at[3], (down, g)),
-    ]
-    for copy in halos:
-        copy.start()
-
-    lax.fori_loop(1, CHIPS - 1, turn, 0)
+    lax.fori_loop(0, CHIPS, turn, 0)
 
     def coefficients(start, live):
         rows = pl.ds(start, 8)
@@ -125,8 +105,22 @@
 
     lax.fori_loop(0, CHIPS, own_coefficients, 0)
 
+    def remote(src, dst, send_sem, recv_sem, device):
+        return pltpu.make_async_remote_copy(
+            src_ref=src, dst_ref=dst, send_sem=send_sem, recv_sem=recv_sem,
+            device_id=device, device_id_type=MESH,
+        )
+
+    halos = [
+        remote(sten_ref.at[:, pl.ds(ROWS - 8, 8), :], sten.at[:, pl.ds(0, 8), :], halo_send.at[0], halo_recv.at[0], (up, g)),
+        remote(sten_ref.at[:, pl.ds(0, 8), :], sten.at[:, pl.ds(ROWS + 8, 8), :], halo_send.at[1], halo_recv.at[1], (down, g)),
+        remote(xt.at[pl.ds(ROWS, 4)], xt.at[pl.ds(0, 4)], halo_send.at[2], halo_recv.at[2], (up, g)),
+        remote(xt.at[pl.ds(4, 4)], xt.at[pl.ds(ROWS + 4, 4)], halo_send.at[3], halo_recv.at[3], (down, g)),
+    ]
+
     def target(i):
-        return lax.rem(chip + 7 * i, CHIPS)
+        d = lax.rem(7 * i, CHIPS)
+        return lax.rem(chip // 4 + d // 4, 4) * 4 + lax.rem(lax.rem(chip, 4) + lax.rem(d, 4), 4)
 
     def early_target(i):
         k = target(i)
@@ -166,6 +160,20 @@
             fwd_send, sem, (s, 2 * k + c),
         ).start()
 
+    def send_first(k, c):
+        send_rows(k, c, 0, 1, fwd_recv.at[0])
+        send_rows(k, c, TILE_ROWS - 1, 1, fwd_recv.at[0])
+
+    def send_later(row, sem):
+        def others(i, carry):
+            k = target(i)
+            for c in range(2):
+                send_rows(k, c, row, 1, sem)
+            return carry
+
+        lax.fori_loop(1, CHIPS, others, 0)
+        send_rows(chip, 1 - core, row, 1, sem)
+
     def first_rows(i, carry):
         @pl.when(i == 5)
         def _():
@@ -184,27 +192,25 @@
 
         k = early_target(i)
         forecast(k)
+
+        @pl.when(i == 1)
+        def _():
+            pl.semaphore_wait(barrier, GROUPS - 1 + 4)
+            for copy in halos:
+                copy.start()
+
         for c in range(2):
-            send_rows(k, c, 0, 2, fwd_recv.at[0])
+            send_first(k, c)
         return carry
 
     lax.fori_loop(1, CHIPS, first_rows, 0)
     forecast(chip)
-    send_rows(chip, 1 - core, 0, 2, fwd_recv.at[0])
+    send_first(chip, 1 - core)
     own = pltpu.make_async_copy(
         fsend.at[pl.ds(g * 4, 4)], fields.at[:, pl.ds(pl.multiple_of(g * MEM, MEM), MEM), :], own_sem.at[0]
     )
     own.start()
-
-    for row in (2, 3):
-        def later_rows(i, carry, row=row):
-            k = target(i)
-            for c in range(2):
-                send_rows(k, c, row, 1, fwd_recv.at[row - 1])
-            return carry
-
-        lax.fori_loop(1, CHIPS, later_rows, 0)
-        send_rows(chip, 1 - core, row, 1, fwd_recv.at[row - 1])
+    send_later(1, fwd_recv.at[1])
 
     load_i.wait()
     scale = 1.0 / ((R + 1.0) * (MEMBERS - 1.0))
@@ -218,34 +224,41 @@
     def split_observed(slot):
         obs_high[slot], obs_low[slot] = split(obs[slot])
 
-    rim_w = [
-        remote(wgt.at[TILE_ROWS], wgt.at[0], rim_send.at[0], rim_recv.at[0], nxt_id),
-        remote(wgt.at[1], wgt.at[TILE_ROWS + 1], rim_send.at[1], rim_recv.at[1], prv_id),
-    ]
-    for copy in rim_w:
-        copy.start()
-    rim_o = [
-        remote(obs.at[TILE_ROWS], obs.at[0], rim_send.at[2], rim_recv.at[2], nxt_id),
-        remote(obs.at[1], obs.at[TILE_ROWS + 1], rim_send.at[3], rim_recv.at[3], prv_id),
-    ]
+    def send_rim(array, src, dst, n, device):
+        def piece(p, carry):
+            part = pl.ds(pl.multiple_of(p * OB, OB), OB)
+            remote(array.at[src, part], array.at[dst, part], rim_send.at[n], rim_recv.at[n], device).start()
+            return carry
+
+        lax.fori_loop(0, ROW_OBS // OB, piece, 0)
+
+    def rim_wait(array, sem):
+        pltpu.make_async_copy(array.at[0], array.at[0], sem).wait()
+
+    send_rim(wgt, TILE_ROWS, 0, 0, nxt_id)
+    send_rim(wgt, 1, TILE_ROWS + 1, 1, prv_id)
 
     for row in range(TILE_ROWS):
         split_weights(row + 1)
 
-    lane = lax.broadcasted_iota(jnp.int32, (OB, 128), 1)
+    square[...] = jnp.zeros_like(square)
+    square[pl.ds(0, TILE_BLOCKS), pl.ds(0, OB)] = cell_ref[...].astype(F32)
+    cells = square[...].T
+    lane = lax.broadcasted_iota(jnp.int32, (OB, 128), 1).astype(F32)
     for b in range(TILE_BLOCKS):
-        pick[b] = jnp.where(lane == cell_ref[:, b : b + 1], 1.0, 0.0).astype(BF16)
-
-    block = lax.broadcasted_iota(jnp.int32, (TILE_BLOCKS, 128), 0)
-    slot_lane = lax.broadcasted_iota(jnp.int32, (TILE_BLOCKS, 128), 1)
+        pick[b] = jnp.where(lane == cells[:OB, b : b + 1], 1.0, 0.0).astype(BF16)
+
+    block = lax.broadcasted_iota(jnp.int32, (128, TILE_BLOCKS), 1)
+    slot_row = lax.broadcasted_iota(jnp.int32, (128, TILE_BLOCKS), 0)
     here = flat * TILE_BLOCKS + block
     row_start = flat * TILE_BLOCKS + jnp.bitwise_and(block, -8) - R
-    total = jnp.zeros((TILE_BLOCKS, 128), F32)
+    total = jnp.zeros((128, TILE_BLOCKS), F32)
     for n in range(R + 1):
-        member_of = band_ref[:, n : n + 1]
-        height = (R + 1.0) - jnp.abs(member_of - here).astype(F32)
-        total = total + jnp.where(slot_lane == member_of - row_start, height, 0.0)
-    taper[...] = total
+        chosen = band_ref[n : n + 1, :]
+        height = (R + 1.0) - jnp.abs(chosen - here).astype(F32)
+        total = total + jnp.where(slot_row == chosen - row_start, height, 0.0)
+    square[:, pl.ds(0, TILE_BLOCKS)] = total
+    taper[...] = square[...].T[:TILE_BLOCKS]
 
     own.wait()
 
@@ -319,34 +332,37 @@
         one(chip, 1 - core)
 
     arrived(0, 2, fwd_recv.at[0])
-    prepare(0)
-    rim_o[1].start()
-    prepare(1)
-    arrived(2, 1, fwd_recv.at[1])
-    prepare(2)
-
-    def finish(t, carry):
-        row = lax.rem(t + 1, TILE_ROWS)
-
-        @pl.when(t == 1)
-        def _():
-            arrived(3, 1, fwd_recv.at[2])
-            prepare(3)
-            rim_o[0].start()
-
-        @pl.when(t == 2)
-        def _():
-            rim_w[1].wait_recv()
-            rim_o[1].wait_recv()
-            split_weights(TILE_ROWS + 1)
-            split_observed(TILE_ROWS + 1)
-
-        @pl.when(t == 3)
-        def _():
-            rim_w[0].wait_recv()
-            rim_o[0].wait_recv()
-            split_weights(0)
-            split_observed(0)
+
+    def prepare_edge(t, carry):
+        prepare(t * (TILE_ROWS - 1))
+        return carry
+
+    lax.fori_loop(0, 2, prepare_edge, 0)
+    send_rim(obs, TILE_ROWS, 0, 2, nxt_id)
+    send_rim(obs, 1, TILE_ROWS + 1, 3, prv_id)
+    send_later(2, fwd_recv.at[2])
+
+    def finish(row, carry):
+        @pl.when(row == 0)
+        def _():
+            arrived(1, 1, fwd_recv.at[1])
+
+        @pl.when(row == 1)
+        def _():
+            arrived(2, 1, fwd_recv.at[2])
+
+        @pl.when(row < 2)
+        def _():
+            prepare(row + 1)
+
+        @pl.when(row == 0)
+        def _():
+            for n in range(2):
+                rim_wait(wgt, rim_recv.at[n])
+                rim_wait(obs, rim_recv.at[n + 2])
+            for slot in (0, TILE_ROWS + 1):
+                split_weights(slot)
+                split_observed(slot)
 
         analyse(row)
         give_back(row)
@@ -358,8 +374,8 @@
         upd.at[:, pl.ds(pl.multiple_of(g * MEM, MEM), MEM), :], ret_ref.at[pl.ds(TILE_ROWS * g, TILE_ROWS)], own_sem.at[1]
     )
     keep.start()
-    for copy in rim_w + rim_o:
-        copy.wait_send()
+    for n in range(4):
+        rim_wait(wgt, rim_send.at[n])
     sent = fsend.at[pl.ds(0, ROWS - 4)]
     pltpu.make_async_copy(sent, sent, fwd_send).wait()
     keep.wait()
@@ -400,6 +416,7 @@
             pltpu.VMEM((TILE_ROWS + 2, MEMBERS, ROW_OBS), BF16),
             pltpu.VMEM((TILE_ROWS + 2, MEMBERS, ROW_OBS), BF16),
             pltpu.VMEM((MEMBERS, TILE_ROWS * ROW_OBS), F32),
+            pltpu.VMEM((128, 128), F32),
             pltpu.VMEM((TILE_BLOCKS, 128), F32),
             pltpu.VMEM((TILE_ROWS, MEMBERS, LON), F32),
             dma((3,)),
@@ -417,7 +434,7 @@
             collective_id=0, has_side_effects=True, vmem_limit_bytes=60 * 2**20
         ),
         name="cycle",
-    )(initial, stencil_numbers, innovations, obs_prec.reshape(1, -1), obs_cell.T, band_idx)
+    )(initial, stencil_numbers, innovations, obs_prec.reshape(1, -1), obs_cell, band_idx.T)
     group = 32
     return pl.pallas_call(
         turn_kernel,
@@ -425,7 +442,7 @@
         out_shape=jax.ShapeDtypeStruct((MEM, ROWS, LON), F32),
         in_specs=[pl.BlockSpec((group, MEM, LON), lambda i: (i, 0, 0))],
         out_specs=pl.BlockSpec((MEM, group, LON), lambda i: (0, i, 0)),
-        compiler_params=pltpu.CompilerParams(vmem_limit_bytes=32 * 2**20),
+        compiler_params=pltpu.CompilerParams(vmem_limit_bytes=60 * 2**20),
         name="turn",
     )(rows)
 

time: 141 us -> 170 us (1.21)
  Pallas kernels: 135 us -> 170 us
  local copies, waits for them, and re-layouts: 4.95 us -> 0 us
    pallas_call x1, Pallas kernels: 133 us -> 165 us  [shards(): pl.pallas_call(cycle_kernel, out_shape=jax.ShapeDtypeStruct((ROWS, MEM, L...]
    unnamed x4 -> x0, local copies, waits for them, and re-layouts: 4.95 us -> none
    pallas_call x1, Pallas kernels: 2.72 us -> 5 us  [shards(): pl.pallas_call(turn_kernel, grid=(ROWS // group,), out_shape=jax.ShapeDty...]
where the time goes in v1:
time: 170 us
  Pallas kernels  170 us (100%)
    pallas_call x1, Pallas kernels, shards(): pl.pallas_call(cycle_kernel, out_shape=jax.ShapeDtypeStruct((ROWS, MEM, L...  165 us
    pallas_call x1, Pallas kernels, shards(): pl.pallas_call(turn_kernel, grid=(ROWS // group,), out_shape=jax.ShapeDty...  5 us

profile of v1, /device:TPU:17, one launch (start us, length us, event | category | flops | bytes accessed | tf_op | source)
XLA Modules:
  0.0 170.0 jit_solution(15374899710781219785)
XLA Ops:
  0.0 165.0 %cycle.1.rows_ref = f32[128,8,1024]{2,1,0:T(8,128)} custom-call(f32[8,128,1024]{2,1,0:T(8,128)} %init_ref.1, f32[3,128,1024]{2,1,0:T(8,128)} %sten_ref.1, f32[256,1024]{1,0:T(8,128)} %inn_ref.1, f32[1,1024]{1,0:T(1,128)} %bitcast.3, s32[32,32]{1,0:T(8,128)} %cell_ref.1, s32[9,32]{1,0:T(8,128)} %bitcast.2), custom_call_target="tpu_custom_call" | custom-call | tf_op jit(solution)/shard_map/cycle/pallas_call | solution.py:395
  165.0 5.0 %turn.1 = f32[8,128,1024]{2,1,0:T(8,128)} custom-call(f32[128,8,1024]{2,1,0:T(8,128)} %cycle.1.rows_ref), custom_call_target="tpu_custom_call" | custom-call | tf_op jit(solution)/shard_map/turn/pallas_call | solution.py:439

commit v2 on v1

--- a/solution.py
+++ b/solution.py
@@ -23,6 +23,7 @@
 ROW_BLOCKS = 8
 TILE_BLOCKS = 32
 ROW_OBS = ROW_BLOCKS * OB
+TURN_ROWS = 16
 
 
 def split(value):
@@ -119,8 +120,7 @@
     ]
 
     def target(i):
-        d = lax.rem(7 * i, CHIPS)
-        return lax.rem(chip // 4 + d // 4, 4) * 4 + lax.rem(lax.rem(chip, 4) + lax.rem(d, 4), 4)
+        return lax.rem(chip + (7 + 2 * core) * i, CHIPS)
 
     def early_target(i):
         k = target(i)
@@ -211,6 +211,7 @@
     )
     own.start()
     send_later(1, fwd_recv.at[1])
+    send_later(2, fwd_recv.at[2])
 
     load_i.wait()
     scale = 1.0 / ((R + 1.0) * (MEMBERS - 1.0))
@@ -235,8 +236,6 @@
     def rim_wait(array, sem):
         pltpu.make_async_copy(array.at[0], array.at[0], sem).wait()
 
-    send_rim(wgt, TILE_ROWS, 0, 0, nxt_id)
-    send_rim(wgt, 1, TILE_ROWS + 1, 1, prv_id)
 
     for row in range(TILE_ROWS):
         split_weights(row + 1)
@@ -284,14 +283,14 @@
         view = fields.at[pl.ds(row, count), pl.ds(0, MEMBERS - MEM), :]
         pltpu.make_async_copy(view, view, sem).wait()
 
-    def analyse(row):
+    def analyse(row, parts=(0, 1, 2), begun=False):
         def columns(c, carry):
             cols = pl.ds(pl.multiple_of(c * 256, 256), 256)
             high = anom_high[row, :, cols]
             low = anom_low[row, :, cols]
             weights = [taper[pl.ds(row * ROW_BLOCKS + c * 2 + b, 1), :] for b in range(2)]
-            total = fields[row, :, cols]
-            for part in range(3):
+            total = (upd if begun else fields)[row, :, cols]
+            for part in parts:
                 slot = row + part
                 cross = dot3(obs_high[slot], obs_low[slot], high, low)
                 spread = jnp.concatenate(
@@ -333,29 +332,27 @@
 
     arrived(0, 2, fwd_recv.at[0])
 
-    def prepare_edge(t, carry):
-        prepare(t * (TILE_ROWS - 1))
-        return carry
-
-    lax.fori_loop(0, 2, prepare_edge, 0)
-    send_rim(obs, TILE_ROWS, 0, 2, nxt_id)
-    send_rim(obs, 1, TILE_ROWS + 1, 3, prv_id)
-    send_later(2, fwd_recv.at[2])
-
-    def finish(row, carry):
-        @pl.when(row == 0)
+    def prepare_first(t, carry):
+        @pl.when(t == 2)
         def _():
             arrived(1, 1, fwd_recv.at[1])
 
-        @pl.when(row == 1)
-        def _():
-            arrived(2, 1, fwd_recv.at[2])
-
-        @pl.when(row < 2)
-        def _():
-            prepare(row + 1)
-
-        @pl.when(row == 0)
+        prepare(jnp.where(t == 1, TILE_ROWS - 1, t // 2))
+        return carry
+
+    lax.fori_loop(0, 3, prepare_first, 0)
+    analyse(1, (0, 1))
+
+    arrived(2, 1, fwd_recv.at[2])
+    for array, n in ((obs, 2), (wgt, 0)):
+        send_rim(array, TILE_ROWS, 0, n, nxt_id)
+        send_rim(array, 1, TILE_ROWS + 1, n + 1, prv_id)
+    prepare(2)
+    analyse(1, (2,), begun=True)
+    give_back(1)
+
+    def finish(t, carry):
+        @pl.when(t == 1)
         def _():
             for n in range(2):
                 rim_wait(wgt, rim_recv.at[n])
@@ -364,11 +361,12 @@
                 split_weights(slot)
                 split_observed(slot)
 
+        row = jnp.where(t == 0, 2, (t - 1) * (TILE_ROWS - 1))
         analyse(row)
         give_back(row)
         return carry
 
-    lax.fori_loop(0, TILE_ROWS, finish, 0)
+    lax.fori_loop(0, 3, finish, 0)
 
     keep = pltpu.make_async_copy(
         upd.at[:, pl.ds(pl.multiple_of(g * MEM, MEM), MEM), :], ret_ref.at[pl.ds(TILE_ROWS * g, TILE_ROWS)], own_sem.at[1]
@@ -384,8 +382,25 @@
     pltpu.make_async_copy(back, back, ret_recv).wait()
 
 
-def turn_kernel(rows_ref, out_ref):
-    out_ref[...] = jnp.swapaxes(rows_ref[...], 0, 1)
+def turn_kernel(rows_ref, out_ref, rows, turned, load_sem, store_sem):
+    def load(n):
+        part = pl.ds(n * TURN_ROWS, TURN_ROWS)
+        return pltpu.make_async_copy(rows_ref.at[part], rows.at[part], load_sem.at[n])
+
+    def store(n):
+        part = pl.ds(n * TURN_ROWS, TURN_ROWS)
+        return pltpu.make_async_copy(turned.at[:, part, :], out_ref.at[:, part, :], store_sem.at[n])
+
+    count = ROWS // TURN_ROWS
+    for n in range(count):
+        load(n).start()
+    for n in range(count):
+        load(n).wait()
+        for start in range(n * TURN_ROWS, (n + 1) * TURN_ROWS, 8):
+            turned[:, pl.ds(start, 8), :] = jnp.swapaxes(rows[pl.ds(start, 8)], 0, 1)
+        store(n).start()
+    for n in range(count):
+        store(n).wait()
 
 
 def shards(initial, stencil_numbers, innovations, obs_prec, obs_cell, band_idx):
@@ -435,13 +450,17 @@
         ),
         name="cycle",
     )(initial, stencil_numbers, innovations, obs_prec.reshape(1, -1), obs_cell, band_idx.T)
-    group = 32
     return pl.pallas_call(
         turn_kernel,
-        grid=(ROWS // group,),
         out_shape=jax.ShapeDtypeStruct((MEM, ROWS, LON), F32),
-        in_specs=[pl.BlockSpec((group, MEM, LON), lambda i: (i, 0, 0))],
-        out_specs=pl.BlockSpec((MEM, group, LON), lambda i: (0, i, 0)),
+        in_specs=[hbm],
+        out_specs=hbm,
+        scratch_shapes=[
+            pltpu.VMEM((ROWS, MEM, LON), F32),
+            pltpu.VMEM((MEM, ROWS, LON), F32),
+            dma((ROWS // TURN_ROWS,)),
+            dma((ROWS // TURN_ROWS,)),
+        ],
         compiler_params=pltpu.CompilerParams(vmem_limit_bytes=60 * 2**20),
         name="turn",
     )(rows)

time: 170 us -> 129 us (0.76)
  Pallas kernels: 170 us -> 128 us
    pallas_call x1, Pallas kernels: 165 us -> 124 us  [shards(): pl.pallas_call(cycle_kernel, out_shape=jax.ShapeDtypeStruct((ROWS, MEM, L...]
where the time goes in v2:
time: 129 us; the launch traced here: 128 us
  Pallas kernels  128 us (99%)
    pallas_call x1, Pallas kernels, shards(): pl.pallas_call(cycle_kernel, out_shape=jax.ShapeDtypeStruct((ROWS, MEM, L...  124 us
    pallas_call x1, Pallas kernels, shards(): pl.pallas_call(turn_kernel, out_shape=jax.ShapeDtypeStruct((MEM, ROWS, LO...  3.43 us

profile of v2, /device:TPU:17, one launch (start us, length us, event | category | flops | bytes accessed | tf_op | source)
XLA Modules:
  0.0 127.9 jit_solution(13505319595425957565)
XLA Ops:
  0.0 124.5 %cycle.1.rows_ref = f32[128,8,1024]{2,1,0:T(8,128)} custom-call(f32[8,128,1024]{2,1,0:T(8,128)} %init_ref.1, f32[3,128,1024]{2,1,0:T(8,128)} %sten_ref.1, f32[256,1024]{1,0:T(8,128)} %inn_ref.1, f32[1,1024]{1,0:T(1,128)} %bitcast.3, s32[32,32]{1,0:T(8,128)} %cell_ref.1, s32[9,32]{1,0:T(8,128)} %bitcast.2), custom_call_target="tpu_custom_call" | custom-call | tf_op jit(solution)/shard_map/cycle/pallas_call | solution.py:410
  124.5 3.4 %turn.1 = f32[8,128,1024]{2,1,0:T(8,128)} custom-call(f32[128,8,1024]{2,1,0:T(8,128)} %cycle.1.rows_ref), custom_call_target="tpu_custom_call" | custom-call | tf_op jit(solution)/shard_map/turn/pallas_call | solution.py:453

commit v3 on v2

--- a/solution.py
+++ b/solution.py
@@ -122,14 +122,6 @@
     def target(i):
         return lax.rem(chip + (7 + 2 * core) * i, CHIPS)
 
-    def early_target(i):
-        k = target(i)
-        edge = 1 - (lax.rem(k + 1, CHIPS) + 14) // 16
-        middle = 1 - (lax.rem(k + 9, CHIPS) + 14) // 16
-        first = 1 - (i + 11) // 16
-        later = ((i + 7) // 16) * (1 - (i + 3) // 16)
-        return lax.rem(k + 8 * (first * edge + later * middle), CHIPS)
-
     def advance(src, src_start, dst, dst_start, count, coef_base, coef_offset):
         for row in range(count):
             centre = src[src_start + row + 1]
@@ -160,38 +152,34 @@
             fwd_send, sem, (s, 2 * k + c),
         ).start()
 
-    def send_first(k, c):
-        send_rows(k, c, 0, 1, fwd_recv.at[0])
-        send_rows(k, c, TILE_ROWS - 1, 1, fwd_recv.at[0])
-
-    def send_later(row, sem):
-        def others(i, carry):
-            k = target(i)
-            for c in range(2):
-                send_rows(k, c, row, 1, sem)
-            return carry
-
-        lax.fori_loop(1, CHIPS, others, 0)
-        send_rows(chip, 1 - core, row, 1, sem)
+    def half(t):
+        row = t * TILE_ROWS
+        advance(xt, row, step_a, 0, 10, row, 5)
+        advance(step_a, 0, step_b, 0, 8, row, 6)
+        advance(step_b, 0, step_a, 0, 6, row, 7)
+        advance(step_a, 0, fsend, row, 4, row, 8)
+
+    def send_row(k, c, row):
+        send_rows(k, c, row, 1, fwd_recv.at[{0: 0, 3: 0, 1: 1, 2: 2}[row]])
+
+    def is_inner(k):
+        return (k > 0) & (k < CHIPS - 1)
 
     def first_rows(i, carry):
-        @pl.when(i == 5)
-        def _():
-            for copy in halos:
-                copy.wait()
-            coefficients(0, jnp.where(s == 0, 0.0, 1.0).astype(F32))
-            coefficients(ROWS + 8, jnp.where(s == SLABS - 1, 0.0, 1.0).astype(F32))
-
-            @pl.when(s == 0)
-            def _():
-                xt[pl.ds(0, 4)] = jnp.zeros((4, MEM, LON), F32)
-
-            @pl.when(s == SLABS - 1)
-            def _():
-                xt[pl.ds(ROWS + 4, 4)] = jnp.zeros((4, MEM, LON), F32)
-
-        k = early_target(i)
-        forecast(k)
+        k = target(i)
+        inner = is_inner(k)
+
+        @pl.when(inner)
+        def _():
+            forecast(k)
+
+        @pl.when(k == 0)
+        def _():
+            half(1)
+
+        @pl.when(k == CHIPS - 1)
+        def _():
+            half(GROUPS - 2)
 
         @pl.when(i == 1)
         def _():
@@ -199,19 +187,74 @@
             for copy in halos:
                 copy.start()
 
-        for c in range(2):
-            send_first(k, c)
+        @pl.when(inner)
+        def _():
+            for c in range(2):
+                send_row(k, c, 0)
+                send_row(k, c, 3)
+
+        @pl.when(jnp.logical_not(inner))
+        def _():
+            for row in (0, 3, 1, 2):
+                send_row(k, 1 - k // (CHIPS - 1), row)
+
         return carry
 
     lax.fori_loop(1, CHIPS, first_rows, 0)
-    forecast(chip)
-    send_first(chip, 1 - core)
+
+    for copy in halos:
+        copy.wait()
+    coefficients(0, jnp.where(s == 0, 0.0, 1.0).astype(F32))
+    coefficients(ROWS + 8, jnp.where(s == SLABS - 1, 0.0, 1.0).astype(F32))
+
+    @pl.when(s == 0)
+    def _():
+        xt[pl.ds(0, 4)] = jnp.zeros((4, MEM, LON), F32)
+
+    @pl.when(s == SLABS - 1)
+    def _():
+        xt[pl.ds(ROWS + 4, 4)] = jnp.zeros((4, MEM, LON), F32)
+
+    half(0)
+    half(GROUPS - 1)
+
+    @pl.when(is_inner(chip))
+    def _():
+        forecast(chip)
+
+    @pl.when(chip == 0)
+    def _():
+        half(1)
+
+    @pl.when(chip == CHIPS - 1)
+    def _():
+        half(GROUPS - 2)
+
+    for row in (0, 3):
+        send_row(chip, 1 - core, row)
     own = pltpu.make_async_copy(
         fsend.at[pl.ds(g * 4, 4)], fields.at[:, pl.ds(pl.multiple_of(g * MEM, MEM), MEM), :], own_sem.at[0]
     )
     own.start()
-    send_later(1, fwd_recv.at[1])
-    send_later(2, fwd_recv.at[2])
+
+    for row, border_rows in ((1, (0, 3)), (2, (1, 2))):
+        def others(i, carry, row=row, border_rows=border_rows):
+            k = target(i)
+
+            @pl.when(is_inner(k))
+            def _():
+                for c in range(2):
+                    send_row(k, c, row)
+
+            @pl.when(jnp.logical_not(is_inner(k)))
+            def _():
+                for border_row in border_rows:
+                    send_row(k, k // (CHIPS - 1), border_row)
+
+            return carry
+
+        lax.fori_loop(1, CHIPS, others, 0)
+        send_row(chip, 1 - core, row)
 
     load_i.wait()
     scale = 1.0 / ((R + 1.0) * (MEMBERS - 1.0))

time: 129 us -> 125 us (0.969)
  the two profiles are of different devices: /device:TPU:17 before, /device:TPU:41 now
where the time goes in v3:
time: 125 us
  Pallas kernels  125 us (100%)
    pallas_call x1, Pallas kernels, shards(): pl.pallas_call(cycle_kernel, out_shape=jax.ShapeDtypeStruct((ROWS, MEM, L...  122 us
    pallas_call x1, Pallas kernels, shards(): pl.pallas_call(turn_kernel, out_shape=jax.ShapeDtypeStruct((MEM, ROWS, LO...  3.43 us

profile of v3, /device:TPU:41, one launch (start us, length us, event | category | flops | bytes accessed | tf_op | source)
XLA Modules:
  0.0 125.1 jit_solution(1533445012790756108)
XLA Ops:
  0.0 121.6 %cycle.1.rows_ref = f32[128,8,1024]{2,1,0:T(8,128)} custom-call(f32[8,128,1024]{2,1,0:T(8,128)} %init_ref.1, f32[3,128,1024]{2,1,0:T(8,128)} %sten_ref.1, f32[256,1024]{1,0:T(8,128)} %inn_ref.1, f32[1,1024]{1,0:T(1,128)} %bitcast.3, s32[32,32]{1,0:T(8,128)} %cell_ref.1, s32[9,32]{1,0:T(8,128)} %bitcast.2), custom_call_target="tpu_custom_call" | custom-call | tf_op jit(solution)/shard_map/cycle/pallas_call | solution.py:453
  121.7 3.4 %turn.1 = f32[8,128,1024]{2,1,0:T(8,128)} custom-call(f32[128,8,1024]{2,1,0:T(8,128)} %cycle.1.rows_ref), custom_call_target="tpu_custom_call" | custom-call | tf_op jit(solution)/shard_map/turn/pallas_call | solution.py:496

commit v4 on v3

--- a/solution.py
+++ b/solution.py
@@ -365,7 +365,7 @@
             ).start()
 
         def others(i, carry):
-            k = target(i)
+            k = target(CHIPS - i)
             for c in range(2):
                 one(k, c)
             return carry

time: 125 us -> 121 us (0.968)
  the two profiles are of different devices: /device:TPU:41 before, /device:TPU:17 now
where the time goes in v4:
time: 121 us; the launch traced here: 119 us
  Pallas kernels  119 us (98%)
    pallas_call x1, Pallas kernels, shards(): pl.pallas_call(cycle_kernel, out_shape=jax.ShapeDtypeStruct((ROWS, MEM, L...  116 us
    pallas_call x1, Pallas kernels, shards(): pl.pallas_call(turn_kernel, out_shape=jax.ShapeDtypeStruct((MEM, ROWS, LO...  3.43 us

profile of v4, /device:TPU:17, one launch (start us, length us, event | category | flops | bytes accessed | tf_op | source)
XLA Modules:
  0.0 119.5 jit_solution(7710682052901376064)
XLA Ops:
  0.0 116.0 %cycle.1.rows_ref = f32[128,8,1024]{2,1,0:T(8,128)} custom-call(f32[8,128,1024]{2,1,0:T(8,128)} %init_ref.1, f32[3,128,1024]{2,1,0:T(8,128)} %sten_ref.1, f32[256,1024]{1,0:T(8,128)} %inn_ref.1, f32[1,1024]{1,0:T(1,128)} %bitcast.3, s32[32,32]{1,0:T(8,128)} %cell_ref.1, s32[9,32]{1,0:T(8,128)} %bitcast.2), custom_call_target="tpu_custom_call" | custom-call | tf_op jit(solution)/shard_map/cycle/pallas_call | solution.py:453
  116.0 3.4 %turn.1 = f32[8,128,1024]{2,1,0:T(8,128)} custom-call(f32[128,8,1024]{2,1,0:T(8,128)} %cycle.1.rows_ref), custom_call_target="tpu_custom_call" | custom-call | tf_op jit(solution)/shard_map/turn/pallas_call | solution.py:496

commit v5 on v4

--- a/solution.py
+++ b/solution.py
@@ -384,10 +384,13 @@
         return carry
 
     lax.fori_loop(0, 3, prepare_first, 0)
+    for array, n in ((wgt, 0),):
+        send_rim(array, TILE_ROWS, 0, n, nxt_id)
+        send_rim(array, 1, TILE_ROWS + 1, n + 1, prv_id)
     analyse(1, (0, 1))
 
     arrived(2, 1, fwd_recv.at[2])
-    for array, n in ((obs, 2), (wgt, 0)):
+    for array, n in ((obs, 2),):
         send_rim(array, TILE_ROWS, 0, n, nxt_id)
         send_rim(array, 1, TILE_ROWS + 1, n + 1, prv_id)
     prepare(2)

time: 121 us -> 117 us (0.967)
  the two profiles are of different devices: /device:TPU:17 before, /device:TPU:1 now
where the time goes in v5:
time: 117 us
  Pallas kernels  117 us (100%)
    pallas_call x1, Pallas kernels, shards(): pl.pallas_call(cycle_kernel, out_shape=jax.ShapeDtypeStruct((ROWS, MEM, L...  114 us
    pallas_call x1, Pallas kernels, shards(): pl.pallas_call(turn_kernel, out_shape=jax.ShapeDtypeStruct((MEM, ROWS, LO...  3.43 us

profile of v5, /device:TPU:1, one launch (start us, length us, event | category | flops | bytes accessed | tf_op | source)
XLA Modules:
  0.0 117.2 jit_solution(6277002982851073326)
XLA Ops:
  0.0 113.8 %cycle.1.rows_ref = f32[128,8,1024]{2,1,0:T(8,128)} custom-call(f32[8,128,1024]{2,1,0:T(8,128)} %init_ref.1, f32[3,128,1024]{2,1,0:T(8,128)} %sten_ref.1, f32[256,1024]{1,0:T(8,128)} %inn_ref.1, f32[1,1024]{1,0:T(1,128)} %bitcast.3, s32[32,32]{1,0:T(8,128)} %cell_ref.1, s32[9,32]{1,0:T(8,128)} %bitcast.2), custom_call_target="tpu_custom_call" | custom-call | tf_op jit(solution)/shard_map/cycle/pallas_call | solution.py:456
  113.8 3.4 %turn.1 = f32[8,128,1024]{2,1,0:T(8,128)} custom-call(f32[128,8,1024]{2,1,0:T(8,128)} %cycle.1.rows_ref), custom_call_target="tpu_custom_call" | custom-call | tf_op jit(solution)/shard_map/turn/pallas_call | solution.py:499
